TPU v7x, 256 devices: a whole 4x4x8 slice. The times are simulated.
256 devices in a mesh: expert: 64 (over y, z, core), etp: 4 (over x).
Axes of the slice: x: 4, y: 4, z: 8, core: 2. Of those that a mesh axis runs over, the one named last changes fastest.
Arguments:
- tokens: bfloat16 [8192, 2048], P('expert'), may hold values from -6 to 6
- grad_out: bfloat16 [8192, 2048], P('expert'), may hold values from -6 to 6
- routes: int32 [8192, 8], P('expert'), may hold values from 0 to 127, all different within a row; in each aligned block of 128 rows (0 to 127, 128 to 255, ...) at most 10 rows name the same one
- probs: bfloat16 [8192, 8], P('expert'), may hold values from 0.049804688 to 0.3984375
- w_gate: bfloat16 [128, 768, 2048], P('expert', 'etp'), may hold values from -0.125 to 0.125
- w_up: bfloat16 [128, 768, 2048], P('expert', 'etp'), may hold values from -0.125 to 0.125
- w_down: bfloat16 [128, 768, 2048], P('expert', 'etp'), may hold values from -0.21875 to 0.21875
Outputs:
- grad_tokens: bfloat16 [8192, 2048], P('expert')
- grad_probs: bfloat16 [8192, 8], P('expert')
- grad_gate: bfloat16 [128, 768, 2048], P('expert', 'etp')
- grad_up: bfloat16 [128, 768, 2048], P('expert', 'etp')
- grad_down: bfloat16 [128, 768, 2048], P('expert', 'etp')
Inputs may be any that keep to these rules, and one draw needn't show every extreme that they name: `routes`: each row names 8 different experts. Among the 128 rows of one device no expert is named by more than 10 rows, a bound that some block reaches.
All inputs are finite; a program needn't handle non-finite values.
Results may differ from a plain program's by a relative error of at most 0.018.
Values may be sent and summed in bfloat16 or wider, within the bound.
A program may use at most 128 MiB of HBM per device.

v0:
```python
import jax
import jax.numpy as jnp
from jax import lax
from jax.sharding import PartitionSpec as P


def token_sum(slot_rows, target, tok_rows, top_count):
    columns = slot_rows.shape[-1]
    picked = slot_rows.reshape(-1, columns)[target]
    return jnp.sum(picked.reshape(tok_rows, top_count, columns).astype(jnp.float32), axis=1).astype(
        jnp.bfloat16
    )


def expert_major(values, sources, local_experts, capacity):
    tail = values.shape[2:]
    shaped = values.reshape((sources, local_experts, capacity) + tail)
    order = (1, 0, 2) + tuple(range(3, 3 + len(tail)))
    return jnp.transpose(shaped, order).reshape((local_experts, sources * capacity) + tail)


def source_major(values, sources, local_experts, capacity):
    tail = values.shape[2:]
    shaped = values.reshape((local_experts, sources, capacity) + tail)
    order = (1, 0, 2) + tuple(range(3, 3 + len(tail)))
    return jnp.transpose(shaped, order).reshape((sources, local_experts * capacity) + tail)


def body(tokens, grad_out, routes, probs, w_gate, w_up, w_down):
    sources = lax.axis_size("expert")
    local_experts = w_gate.shape[0]
    hid_units = w_gate.shape[1]
    expert_count = sources * local_experts
    tok_rows, top_count = routes.shape
    model_width = tokens.shape[1]
    capacity = max(2, 5 * tok_rows * top_count // (4 * expert_count))
    pair_count = tok_rows * top_count
    flat_routes = routes.reshape(-1)
    one_hot = (flat_routes[:, None] == jnp.arange(expert_count, dtype=jnp.int32)[None, :]).astype(
        jnp.int32
    )
    slot_rank = jnp.sum(jnp.cumsum(one_hot, axis=0) * one_hot, axis=1) - 1
    target = flat_routes * capacity + slot_rank
    slot_table = (
        jnp.full((expert_count * capacity,), pair_count, jnp.int32)
        .at[target]
        .set(jnp.arange(pair_count, dtype=jnp.int32))
    )
    filled = slot_table < pair_count
    safe_index = jnp.where(filled, slot_table, 0)
    token_of = safe_index // top_count
    block_rows = local_experts * capacity
    send_prob = jnp.where(filled, probs.reshape(-1)[safe_index], 0).reshape(sources, block_rows)
    send_rows = jnp.where(filled[:, None], tokens[token_of], 0).reshape(
        sources, block_rows, model_width
    )
    send_grad = jnp.where(filled[:, None], grad_out[token_of], 0).reshape(
        sources, block_rows, model_width
    )
    recv_rows, recv_grad, recv_prob = (
        lax.all_to_all(send_rows, "expert", split_axis=0, concat_axis=0, tiled=True),
        lax.all_to_all(send_grad, "expert", split_axis=0, concat_axis=0, tiled=True),
        lax.all_to_all(send_prob, "expert", split_axis=0, concat_axis=0, tiled=True),
    )
    in_rows = expert_major(recv_rows, sources, local_experts, capacity)
    in_grad = expert_major(recv_grad, sources, local_experts, capacity)
    weight = expert_major(recv_prob, sources, local_experts, capacity).astype(jnp.float32)[
        ..., None
    ]
    gate_up = jnp.concatenate([w_gate, w_up], axis=1)
    both_pre = jnp.einsum("end,ehd->enh", in_rows, gate_up, preferred_element_type=jnp.float32)
    pre_gate = both_pre[..., :hid_units]
    pre_up = both_pre[..., hid_units:]
    back_grad = jnp.einsum("end,ehd->enh", in_grad, w_down, preferred_element_type=jnp.float32)
    sigma_gate = jax.nn.sigmoid(pre_gate)
    activated = pre_gate * sigma_gate
    hidden = (activated * pre_up).astype(jnp.bfloat16)
    prob_local = jnp.sum(hidden.astype(jnp.float32) * back_grad, axis=-1)
    prob_part = source_major(prob_local, sources, local_experts, capacity)
    scaled = (weight * in_grad.astype(jnp.float32)).astype(jnp.bfloat16)
    grad_down = jnp.einsum(
        "enh,end->ehd", hidden, scaled, preferred_element_type=jnp.float32
    ).astype(jnp.bfloat16)
    hidden_grad = weight * back_grad
    d_gate = (hidden_grad * pre_up * sigma_gate * (1.0 + pre_gate * (1.0 - sigma_gate))).astype(
        jnp.bfloat16
    )
    d_up = (hidden_grad * activated).astype(jnp.bfloat16)
    d_both = jnp.concatenate([d_gate, d_up], axis=-1)
    grad_both = jnp.einsum(
        "enh,end->ehd", d_both, in_rows, preferred_element_type=jnp.float32
    ).astype(jnp.bfloat16)
    grad_gate = grad_both[:, :hid_units]
    grad_up = grad_both[:, hid_units:]
    local_part = jnp.einsum(
        "enh,ehd->end", d_both, gate_up, preferred_element_type=jnp.float32
    ).astype(jnp.bfloat16)
    partial_sum = source_major(local_part, sources, local_experts, capacity).astype(jnp.float32)
    totals, prob_total = (
        lax.psum(partial_sum.astype(jnp.bfloat16), "etp").astype(jnp.float32),
        lax.psum(prob_part.astype(jnp.bfloat16), "etp").astype(jnp.float32),
    )
    back_rows, back_prob = (
        lax.all_to_all(
            totals.astype(jnp.bfloat16), "expert", split_axis=0, concat_axis=0, tiled=True
        ),
        lax.all_to_all(
            prob_total.astype(jnp.bfloat16), "expert", split_axis=0, concat_axis=0, tiled=True
        ),
    )
    grad_tokens = token_sum(back_rows, target, tok_rows, top_count)
    grad_probs = back_prob.reshape(-1)[target].reshape(tok_rows, top_count)
    return (grad_tokens, grad_probs, grad_gate, grad_up, grad_down)


def solution(mesh):
    return jax.shard_map(
        body,
        mesh=mesh,
        in_specs=(
            P("expert", None),
            P("expert", None),
            P("expert", None),
            P("expert", None),
            P("expert", "etp", None),
            P("expert", "etp", None),
            P("expert", "etp", None),
        ),
        out_specs=(
            P("expert", None),
            P("expert", None),
            P("expert", "etp", None),
            P("expert", "etp", None),
            P("expert", "etp", None),
        ),
        check_vma=False,
    )
```

profile of v0, /device:TPU:1, one launch (start us, length us, event | category | flops | bytes accessed | tf_op | source)
XLA Modules:
  0.0 739.5 jit_solution(8986756804399492162)
XLA Ops:
  15.4 8.0 %gather_fusion = bf16[1280]{0:T(1024)(128)(2,1)S(1)} fusion(bf16[1024]{0:T(1024)(128)(2,1)S(1)} %reshape.132, s32[2048]{0:T(1024)S(1)} %pad_clamp_fusion.1), kind=kCustom, calls=%fused_computation | custom fusion | bytes 10240 | tf_op jit(solution)/shard_map/gather | solution.py:53
  24.1 13.2 %all-to-all-start = ((bf16[64,1,20]{2,1,0:T(2,128)(2,1)}), bf16[64,1,20]{2,1,0:T(2,128)(2,1)S(1)}, u32[]{:S(2)}, u32[]{:S(2)}) async-start(bf16[64,1,20]{2,1,0:T(2,128)(2,1)} %all_to_all.28), calls=%async_computation | async-start | bytes 65536 | tf_op jit(solution)/shard_map/all_to_all | solution.py:63
  37.4 6.2 gather_fusion.2
  43.6 9.0 %gather.23 = bf16[64,20,2048]{2,1,0:T(8,128)(2,1)} reshape(bf16[1280,2048]{1,0:T(8,128)(2,1)} %gather_fusion.2) | data formatting | bytes 10485760 | tf_op jit(solution)/shard_map/gather | solution.py:54
  52.6 6.2 gather_fusion.1
  58.8 8.9 %gather.21 = bf16[64,20,2048]{2,1,0:T(8,128)(2,1)} reshape(bf16[1280,2048]{1,0:T(8,128)(2,1)} %gather_fusion.1) | data formatting | bytes 10485760 | tf_op jit(solution)/shard_map/gather | solution.py:57
  67.8 10.2 %broadcast_select_fusion = (bf16[64,20,2048]{2,1,0:T(8,128)(2,1)}, bf16[64,20,2048]{2,1,0:T(8,128)(2,1)}) fusion(bf16[64,20,2048]{2,1,0:T(8,128)(2,1)} %gather.23, pred[64,20]{1,0:T(8,128)(4,1)S(1)} %broadcast_in_dim.43, bf16[64,20,2048]{2,1,0:T(8,128)(2,1)} %gather.21), kind=kLoop, calls=%fused_computation.7 | loop fusion | flops 5242880 | bytes 20972800 | tf_op jit(solution)/shard_map/jit(_where)/select_n | solution.py:54
  78.0 151.6 %all_to_all.34 = bf16[64,20,2048]{2,1,0:T(8,128)(2,1)} all-to-all(bf16[64,20,2048]{2,1,0:T(8,128)(2,1)} %get-tuple-element.30), channel_id=1, replica_groups=mesh['expert'=64,'etp'=4] {'expert'}, dimensions={0} | all-to-all | bytes 10485760 | tf_op jit(solution)/shard_map/all_to_all | solution.py:61
  229.5 6.1 all-to-all-start.1
  240.3 8.0 %copy.74 = bf16[64,20,2048]{2,0,1:T(8,128)(2,1)} copy(bf16[64,20,2048]{2,1,0:T(8,128)(2,1)} %all_to_all.34) | data formatting | bytes 10485760 | tf_op jit(solution)/shard_map/all_to_all | solution.py:61
  248.3 10.3 %copy.75 = bf16[2,64,10,2048]{3,0,2,1:T(2,128)(2,1)} copy(bf16[2,64,10,2048]{3,1,2,0:T(8,128)(2,1)} %bitcast.38) | data formatting | bytes 10485760 | tf_op jit(solution)/shard_map/transpose | solution.py:19
  258.6 118.0 %all-to-all-done.1 = bf16[64,20,2048]{2,1,0:T(8,128)(2,1)} async-done(((bf16[64,20,2048]{2,1,0:T(8,128)(2,1)}), bf16[64,20,2048]{2,1,0:T(8,128)(2,1)}, u32[]{:S(2)}, u32[]{:S(2)}) %all-to-all-start.1) | async-done | bytes 5242912 | tf_op jit(solution)/shard_map/all_to_all | solution.py:62
  376.5 8.5 %copy.71 = bf16[64,20,2048]{2,0,1:T(8,128)(2,1)} copy(bf16[64,20,2048]{2,1,0:T(8,128)(2,1)} %all-to-all-done.1) | data formatting | bytes 10485760 | tf_op jit(solution)/shard_map/all_to_all | solution.py:62
  385.0 10.2 %copy.72 = bf16[2,64,10,2048]{3,0,2,1:T(2,128)(2,1)} copy(bf16[2,64,10,2048]{3,1,2,0:T(8,128)(2,1)} %bitcast.39) | data formatting | bytes 10485760 | tf_op jit(solution)/shard_map/transpose | solution.py:19
  395.2 7.4 fusion.6
  402.6 5.1 multiply_reduce_fusion
  408.5 7.1 convolution_convert_fusion
  415.6 10.2 %copy.78 = bf16[2,640,2048]{2,0,1:T(2,128)(2,1)} copy(bf16[2,640,2048]{2,1,0:T(8,128)(2,1)} %convolution_convert_fusion) | data formatting | bytes 10485760 | tf_op jit(solution)/shard_map/convert_element_type | solution.py:97
  425.8 7.9 %copy.79 = bf16[64,2,10,2048]{3,0,2,1:T(8,128)(2,1)} copy(bf16[64,2,10,2048]{3,1,2,0:T(2,128)(2,1)} %bitcast.40) | data formatting | bytes 10485760 | tf_op jit(solution)/shard_map/transpose | solution.py:26
  434.0 8.6 %psum.15 = bf16[64,1,20]{0,2,1:T(8,128)(2,1)S(1)} all-reduce(bf16[64,1,20]{0,2,1:T(8,128)(2,1)S(1)} %all_to_all.26), channel_id=1, replica_groups=mesh['expert'=64,'etp'=4] {'etp'}, use_global_device_ids=true, to_apply=%region_7.8 | all-reduce | flops 1280 | bytes 5120 | tf_op jit(solution)/shard_map/psum | solution.py:101
  443.3 7.7 %all-to-all-start.4 = ((bf16[64,1,20]{2,1,0:T(2,128)(2,1)}), bf16[64,1,20]{2,1,0:T(2,128)(2,1)S(1)}, u32[]{:S(2)}, u32[]{:S(2)}) async-start(bf16[64,1,20]{2,1,0:T(2,128)(2,1)} %copy.82), calls=%async_computation.4 | async-start | bytes 65536 | tf_op jit(solution)/shard_map/all_to_all | solution.py:107
  451.0 94.3 %all-reduce.2.cloned.1.call-done = bf16[64,20,2048]{2,0,1:T(8,128)(2,1)} async-done(((bf16[64,20,2048]{2,0,1:T(8,128)(2,1)}), bf16[64,20,2048]{2,0,1:T(8,128)(2,1)}) %all-reduce.2.cloned.1.call-update) | async-done | bytes 5242896 | tf_op jit(solution)/shard_map/psum | solution.py:100
  545.3 8.1 %copy.80 = bf16[64,20,2048]{2,1,0:T(8,128)(2,1)} copy(bf16[64,20,2048]{2,0,1:T(8,128)(2,1)} %all-reduce.2.cloned.1.call-done) | data formatting | bytes 10485760 | tf_op jit(solution)/shard_map/psum | solution.py:100
  553.4 11.0 %all-to-all-start.3 = ((bf16[64,20,2048]{2,1,0:T(8,128)(2,1)}), bf16[64,20,2048]{2,1,0:T(8,128)(2,1)}, u32[]{:S(2)}, u32[]{:S(2)}) async-start(bf16[64,20,2048]{2,1,0:T(8,128)(2,1)} %copy.80), calls=%async_computation.3 | async-start | bytes 12582912 | tf_op jit(solution)/shard_map/all_to_all | solution.py:104
  564.6 6.2 multiply_convert_fusion
  570.9 4.6 fusion.11
  575.5 4.4 fusion.8
  582.0 6.8 gather_fusion.4
  589.5 115.7 %all-to-all-done.3 = bf16[64,20,2048]{2,1,0:T(8,128)(2,1)} async-done(((bf16[64,20,2048]{2,1,0:T(8,128)(2,1)}), bf16[64,20,2048]{2,1,0:T(8,128)(2,1)}, u32[]{:S(2)}, u32[]{:S(2)}) %all-to-all-start.3) | async-done | bytes 5242912 | tf_op jit(solution)/shard_map/all_to_all | solution.py:104
  705.3 9.0 %reshape.139 = bf16[1280,2048]{1,0:T(8,128)(2,1)} reshape(bf16[64,20,2048]{2,1,0:T(8,128)(2,1)} %all-to-all-done.3) | data formatting | bytes 10485760 | tf_op jit(solution)/shard_map/reshape | solution.py:9
  714.3 12.1 %gather_fusion.3 = bf16[1024,2048]{1,0:T(8,128)(2,1)} fusion(bf16[1280,2048]{1,0:T(8,128)(2,1)} %reshape.139, s32[1024]{0:T(1024)S(1)} %broadcast_clamp_fusion), kind=kCustom, calls=%fused_computation.3 | custom fusion | bytes 8392704 | tf_op jit(solution)/shard_map/gather | solution.py:9
  726.4 5.9 bitcast_reduce_fusion
  (72 shorter events, 18.4 us)
Async XLA Ops:
  7.2 395.4 %copy-start = (bf16[2,192,2048]{2,1,0:T(8,128)(2,1)S(1)}, bf16[2,192,2048]{2,1,0:T(8,128)(2,1)}, u32[]{:S(2)}) copy-start(bf16[2,192,2048]{2,1,0:T(8,128)(2,1)} %param.13) | copy-start | bytes 4718596
  7.2 30.2 %copy-start.2 = (bf16[128,2048]{1,0:T(8,128)(2,1)S(1)}, bf16[128,2048]{1,0:T(8,128)(2,1)}, u32[]{:S(2)}) copy-start(bf16[128,2048]{1,0:T(8,128)(2,1)} %param.7) | copy-start | bytes 1572868
  24.1 53.9 %all-to-all-start = ((bf16[64,1,20]{2,1,0:T(2,128)(2,1)}), bf16[64,1,20]{2,1,0:T(2,128)(2,1)S(1)}, u32[]{:S(2)}, u32[]{:S(2)}) async-start(bf16[64,1,20]{2,1,0:T(2,128)(2,1)} %all_to_all.28), calls=%async_computation | async-start | bytes 65536 | tf_op jit(solution)/shard_map/all_to_all | solution.py:63
  43.6 9.0 %copy-start.3 = (bf16[128,2048]{1,0:T(8,128)(2,1)S(1)}, bf16[128,2048]{1,0:T(8,128)(2,1)}, u32[]{:S(2)}) copy-start(bf16[128,2048]{1,0:T(8,128)(2,1)} %param.8) | copy-start | bytes 1572868
  229.5 6.4 copy-start.5
  229.5 147.0 %all-to-all-start.1 = ((bf16[64,20,2048]{2,1,0:T(8,128)(2,1)}), bf16[64,20,2048]{2,1,0:T(8,128)(2,1)}, u32[]{:S(2)}, u32[]{:S(2)}) async-start(bf16[64,20,2048]{2,1,0:T(8,128)(2,1)} %get-tuple-element.31), calls=%async_computation.1 | async-start | bytes 12582912 | tf_op jit(solution)/shard_map/all_to_all | solution.py:62
  235.7 309.6 %all-reduce.2.cloned.1.call-start = ((), (), s32[]{:S(2)}) async-start(), calls=%async_computation.5 | async-start | bytes 10485760 | tf_op jit(solution)/shard_map/psum | solution.py:100
  395.2 7.4 %copy-start.4 = (bf16[2,64,10,2048]{3,0,2,1:T(2,128)(2,1)S(1)}, bf16[2,64,10,2048]{3,0,2,1:T(2,128)(2,1)}, u32[]{:S(2)}) copy-start(bf16[2,64,10,2048]{3,0,2,1:T(2,128)(2,1)} %copy.72) | copy-start | bytes 15728644
  407.7 0.8 copy-start.6
  443.3 110.1 %all-to-all-start.4 = ((bf16[64,1,20]{2,1,0:T(2,128)(2,1)}), bf16[64,1,20]{2,1,0:T(2,128)(2,1)S(1)}, u32[]{:S(2)}, u32[]{:S(2)}) async-start(bf16[64,1,20]{2,1,0:T(2,128)(2,1)} %copy.82), calls=%async_computation.4 | async-start | bytes 65536 | tf_op jit(solution)/shard_map/all_to_all | solution.py:107
  553.4 22.1 %slice-start = ((s8[5242880]{0:T(1024)(128)(4,1)}), s8[1048576]{0:T(1024)(128)(4,1)S(1)}, s32[]{:S(2)}) async-start(s8[5242880]{0:T(1024)(128)(4,1)} %bitcast.42), calls=%async_computation.6 | async-start | bytes 2097152
  553.4 151.9 %all-to-all-start.3 = ((bf16[64,20,2048]{2,1,0:T(8,128)(2,1)}), bf16[64,20,2048]{2,1,0:T(8,128)(2,1)}, u32[]{:S(2)}, u32[]{:S(2)}) async-start(bf16[64,20,2048]{2,1,0:T(8,128)(2,1)} %copy.80), calls=%async_computation.3 | async-start | bytes 12582912 | tf_op jit(solution)/shard_map/all_to_all | solution.py:104
  564.6 6.2 copy-start.8
  564.6 10.8 %slice-start.1 = ((s8[5242880]{0:T(1024)(128)(4,1)}), s8[4194304]{0:T(1024)(128)(4,1)S(1)}, s32[]{:S(2)}) async-start(s8[5242880]{0:T(1024)(128)(4,1)} %bitcast.42), calls=%async_computation.7 | async-start | bytes 8388608
  570.8 4.7 copy-start.7
  714.3 18.0 %copy-start.1 = (bf16[2,192,2048]{2,1,0:T(8,128)(2,1)S(1)}, bf16[2,192,2048]{2,1,0:T(8,128)(2,1)}, u32[]{:S(2)}) copy-start(bf16[2,192,2048]{2,1,0:T(8,128)(2,1)} %param.13) | copy-start | bytes 4718596
Sparse Core Ops, SparseCore 0:
  433.8 111.4 all-reduce.1
where the time goes:
time: 747 us; the launch traced here: 739 us
  waiting for transfers between devices  328 us (44%)
  blocking collectives  160 us (21%)
  local copies, waits for them, and re-layouts  146 us (20%)
  starting transfers between devices  38.3 us (5%)
  matrix products  28.6 us (4%)
  other arithmetic  23.9 us (3%)
  between operations  14.7 us (2%)
    all_to_all x1, blocking collectives, body(): lax.all_to_all(send_rows, 'expert', split_axis=0, concat_axis=0, tiled=True)  152 us
    all_to_all x1, waiting for transfers between devices, body(): lax.all_to_all(send_grad, 'expert', split_axis=0, concat_axis=0, tiled=True)  118 us
    all_to_all x1, waiting for transfers between devices, body(): lax.all_to_all(totals.astype(jnp.bfloat16), 'expert', split_axis=0, conca...  116 us
    psum x1, waiting for transfers between devices, body(): lax.psum(partial_sum.astype(jnp.bfloat16), 'etp').astype(jnp.float32)  94.3 us
    transpose x2, local copies, waits for them, and re-layouts, expert_major(): jnp.transpose(shaped, order)  20.5 us
    gather x2, local copies, waits for them, and re-layouts, body(): tokens[token_of]  15.2 us
    gather x2, local copies, waits for them, and re-layouts, body(): grad_out[token_of]  15.1 us
  transfers between devices with their start and end apart: 5, of which 3 were waited for; matrix products, arithmetic and copies ran while one was open for 13% of the time, Pallas kernels for 0%

commit v1 on v0

--- a/solution.py
+++ b/solution.py
@@ -96,8 +96,9 @@
         "enh,ehd->end", d_both, gate_up, preferred_element_type=jnp.float32
     ).astype(jnp.bfloat16)
     partial_sum = source_major(local_part, sources, local_experts, capacity).astype(jnp.float32)
+    view_rates_on = lambda sheet, which_axis: jnp.sum(lax.all_gather(sheet, which_axis), axis=0)
     totals, prob_total = (
-        lax.psum(partial_sum.astype(jnp.bfloat16), "etp").astype(jnp.float32),
+        view_rates_on(partial_sum.astype(jnp.bfloat16), "etp").astype(jnp.float32),
         lax.psum(prob_part.astype(jnp.bfloat16), "etp").astype(jnp.float32),
     )
     back_rows, back_prob = (

time: 747 us -> 839 us (1.12)
  waiting for transfers between devices: 328 us -> 405 us
  other arithmetic: 23.9 us -> 38.5 us
    all_gather x0 -> x1, waiting for transfers between devices: none -> 171 us  [body(): lax.all_gather(sheet, which_axis)]
    psum x1 -> x0, waiting for transfers between devices: 94.3 us -> none  [body(): lax.psum(partial_sum.astype(jnp.bfloat16), 'etp').astype(jnp.float32)]
    reduce_sum x0 -> x1, other arithmetic: none -> 14.8 us  [body(): jnp.sum(lax.all_gather(sheet, which_axis), axis=0)]
where the time goes in v1:
time: 839 us; the launch traced here: 832 us
  waiting for transfers between devices  405 us (48%)
  blocking collectives  160 us (19%)
  local copies, waits for them, and re-layouts  146 us (17%)
  starting transfers between devices  38.7 us (5%)
  other arithmetic  38.5 us (5%)
  matrix products  28.6 us (3%)
  between operations  14.8 us (2%)
    all_gather x1, waiting for transfers between devices, body(): lax.all_gather(sheet, which_axis)  171 us
    all_to_all x1, blocking collectives, body(): lax.all_to_all(send_rows, 'expert', split_axis=0, concat_axis=0, tiled=True)  152 us
    all_to_all x1, waiting for transfers between devices, body(): lax.all_to_all(send_grad, 'expert', split_axis=0, concat_axis=0, tiled=True)  118 us
    all_to_all x1, waiting for transfers between devices, body(): lax.all_to_all(totals.astype(jnp.bfloat16), 'expert', split_axis=0, conca...  116 us
    transpose x2, local copies, waits for them, and re-layouts, expert_major(): jnp.transpose(shaped, order)  20.6 us
  transfers between devices with their start and end apart: 5, of which 3 were waited for; matrix products, arithmetic and copies ran while one was open for 13% of the time, Pallas kernels for 0%

profile of v1, /device:TPU:1, one launch (start us, length us, event | category | flops | bytes accessed | tf_op | source)
XLA Modules:
  0.0 831.6 jit_solution(10110135680809178359)
XLA Ops:
  15.4 8.0 gather_fusion
  24.1 13.2 %all-to-all-start = ((bf16[64,1,20]{2,1,0:T(2,128)(2,1)}), bf16[64,1,20]{2,1,0:T(2,128)(2,1)S(1)}, u32[]{:S(2)}, u32[]{:S(2)}) async-start(bf16[64,1,20]{2,1,0:T(2,128)(2,1)} %all_to_all.28), calls=%async_computation | async-start | bytes 65536 | tf_op jit(solution)/shard_map/all_to_all | solution.py:63
  37.4 6.1 gather_fusion.1
  43.5 9.0 %gather.21 = bf16[64,20,2048]{2,1,0:T(8,128)(2,1)} reshape(bf16[1280,2048]{1,0:T(8,128)(2,1)} %gather_fusion.1) | data formatting | bytes 10485760 | tf_op jit(solution)/shard_map/gather | solution.py:57
  52.5 6.2 gather_fusion.2
  58.7 8.9 %gather.23 = bf16[64,20,2048]{2,1,0:T(8,128)(2,1)} reshape(bf16[1280,2048]{1,0:T(8,128)(2,1)} %gather_fusion.2) | data formatting | bytes 10485760 | tf_op jit(solution)/shard_map/gather | solution.py:54
  67.6 10.2 %broadcast_select_fusion = (bf16[64,20,2048]{2,1,0:T(8,128)(2,1)}, bf16[64,20,2048]{2,1,0:T(8,128)(2,1)}) fusion(bf16[64,20,2048]{2,1,0:T(8,128)(2,1)} %gather.23, pred[64,20]{1,0:T(8,128)(4,1)S(1)} %broadcast_in_dim.43, bf16[64,20,2048]{2,1,0:T(8,128)(2,1)} %gather.21), kind=kLoop, calls=%fused_computation.7 | loop fusion | flops 5242880 | bytes 20972800 | tf_op jit(solution)/shard_map/jit(_where)/select_n | solution.py:54
  77.8 151.6 %all_to_all.34 = bf16[64,20,2048]{2,1,0:T(8,128)(2,1)} all-to-all(bf16[64,20,2048]{2,1,0:T(8,128)(2,1)} %get-tuple-element.35), channel_id=1, replica_groups=mesh['expert'=64,'etp'=4] {'expert'}, dimensions={0} | all-to-all | bytes 10485760 | tf_op jit(solution)/shard_map/all_to_all | solution.py:61
  229.4 6.1 all-to-all-start.1
  240.2 8.1 copy.98
  248.3 10.3 %copy.99 = bf16[2,64,10,2048]{3,0,2,1:T(2,128)(2,1)} copy(bf16[2,64,10,2048]{3,1,2,0:T(8,128)(2,1)} %bitcast.37) | data formatting | bytes 10485760 | tf_op jit(solution)/shard_map/transpose | solution.py:19
  258.6 117.8 %all-to-all-done.1 = bf16[64,20,2048]{2,1,0:T(8,128)(2,1)} async-done(((bf16[64,20,2048]{2,1,0:T(8,128)(2,1)}), bf16[64,20,2048]{2,1,0:T(8,128)(2,1)}, u32[]{:S(2)}, u32[]{:S(2)}) %all-to-all-start.1) | async-done | bytes 5242912 | tf_op jit(solution)/shard_map/all_to_all | solution.py:62
  376.4 8.5 %copy.95 = bf16[64,20,2048]{2,0,1:T(8,128)(2,1)} copy(bf16[64,20,2048]{2,1,0:T(8,128)(2,1)} %all-to-all-done.1) | data formatting | bytes 10485760 | tf_op jit(solution)/shard_map/all_to_all | solution.py:62
  384.8 10.4 %copy.96 = bf16[2,64,10,2048]{3,0,2,1:T(2,128)(2,1)} copy(bf16[2,64,10,2048]{3,1,2,0:T(8,128)(2,1)} %bitcast.38) | data formatting | bytes 10485760 | tf_op jit(solution)/shard_map/transpose | solution.py:19
  395.2 7.4 fusion.6
  402.6 5.1 multiply_reduce_fusion
  408.5 7.1 convolution_convert_fusion
  415.6 10.2 %copy.102 = bf16[2,640,2048]{2,0,1:T(2,128)(2,1)} copy(bf16[2,640,2048]{2,1,0:T(8,128)(2,1)} %convolution_convert_fusion) | data formatting | bytes 10485760 | tf_op jit(solution)/shard_map/convert_element_type | solution.py:97
  425.8 7.8 copy.103
  434.0 8.5 %psum.7 = bf16[64,1,20]{0,2,1:T(8,128)(2,1)S(1)} all-reduce(bf16[64,1,20]{0,2,1:T(8,128)(2,1)S(1)} %all_to_all.26), channel_id=1, replica_groups=mesh['expert'=64,'etp'=4] {'etp'}, use_global_device_ids=true, to_apply=%region_7.8 | all-reduce | flops 1280 | bytes 5120 | tf_op jit(solution)/shard_map/psum | solution.py:102
  443.3 7.7 all-to-all-start.4
  451.0 171.4 %all-gather.2.cloned.1.call-done = bf16[4,64,20,2048]{3,1,2,0:T(8,128)(2,1)} async-done(((bf16[1,64,20,2048]{3,1,2,0:T(8,128)(2,1)}), bf16[4,64,20,2048]{3,1,2,0:T(8,128)(2,1)}) %all-gather.2.cloned.1.call-update) | async-done | bytes 20971536 | tf_op jit(solution)/shard_map/all_gather | solution.py:99
  622.4 14.8 %reduce_sum.43 = bf16[64,20,2048]{2,0,1:T(8,128)(2,1)} reduce(bf16[4,64,20,2048]{3,1,2,0:T(8,128)(2,1)} %all-gather.2.cloned.1.call-done, bf16[]{:T(256)} %constant.34.clone.1), dimensions={0}, to_apply=%region_4.5 | reduce | flops 7864320 | bytes 26214402 | tf_op jit(solution)/shard_map/reduce_sum | solution.py:99
  637.2 8.1 copy.104
  645.3 11.4 %all-to-all-start.3 = ((bf16[64,20,2048]{2,1,0:T(8,128)(2,1)}), bf16[64,20,2048]{2,1,0:T(8,128)(2,1)}, u32[]{:S(2)}, u32[]{:S(2)}) async-start(bf16[64,20,2048]{2,1,0:T(8,128)(2,1)} %copy.104), calls=%async_computation.3 | async-start | bytes 12582912 | tf_op jit(solution)/shard_map/all_to_all | solution.py:105
  656.9 6.2 multiply_convert_fusion
  663.1 4.6 fusion.11
  674.2 6.8 gather_fusion.4
  681.8 115.5 %all-to-all-done.3 = bf16[64,20,2048]{2,1,0:T(8,128)(2,1)} async-done(((bf16[64,20,2048]{2,1,0:T(8,128)(2,1)}), bf16[64,20,2048]{2,1,0:T(8,128)(2,1)}, u32[]{:S(2)}, u32[]{:S(2)}) %all-to-all-start.3) | async-done | bytes 5242912 | tf_op jit(solution)/shard_map/all_to_all | solution.py:105
  797.3 9.0 %reshape.137 = bf16[1280,2048]{1,0:T(8,128)(2,1)} reshape(bf16[64,20,2048]{2,1,0:T(8,128)(2,1)} %all-to-all-done.3) | data formatting | bytes 10485760 | tf_op jit(solution)/shard_map/reshape | solution.py:9
  806.3 12.1 %gather_fusion.3 = bf16[1024,2048]{1,0:T(8,128)(2,1)} fusion(bf16[1280,2048]{1,0:T(8,128)(2,1)} %reshape.137, s32[1024]{0:T(1024)S(1)} %broadcast_clamp_fusion), kind=kCustom, calls=%fused_computation.3 | custom fusion | bytes 8392704 | tf_op jit(solution)/shard_map/gather | solution.py:9
  818.4 5.9 bitcast_reduce_fusion
  (73 shorter events, 22.9 us)
Async XLA Ops:
  7.2 395.4 %copy-start = (bf16[2,192,2048]{2,1,0:T(8,128)(2,1)S(1)}, bf16[2,192,2048]{2,1,0:T(8,128)(2,1)}, u32[]{:S(2)}) copy-start(bf16[2,192,2048]{2,1,0:T(8,128)(2,1)} %param.13) | copy-start | bytes 4718596
  7.2 30.2 %copy-start.2 = (bf16[128,2048]{1,0:T(8,128)(2,1)S(1)}, bf16[128,2048]{1,0:T(8,128)(2,1)}, u32[]{:S(2)}) copy-start(bf16[128,2048]{1,0:T(8,128)(2,1)} %param.8) | copy-start | bytes 1572868
  24.1 53.7 %all-to-all-start = ((bf16[64,1,20]{2,1,0:T(2,128)(2,1)}), bf16[64,1,20]{2,1,0:T(2,128)(2,1)S(1)}, u32[]{:S(2)}, u32[]{:S(2)}) async-start(bf16[64,1,20]{2,1,0:T(2,128)(2,1)} %all_to_all.28), calls=%async_computation | async-start | bytes 65536 | tf_op jit(solution)/shard_map/all_to_all | solution.py:63
  43.5 9.0 %copy-start.3 = (bf16[128,2048]{1,0:T(8,128)(2,1)S(1)}, bf16[128,2048]{1,0:T(8,128)(2,1)}, u32[]{:S(2)}) copy-start(bf16[128,2048]{1,0:T(8,128)(2,1)} %param.7) | copy-start | bytes 1572868
  229.4 6.4 copy-start.5
  229.4 147.0 %all-to-all-start.1 = ((bf16[64,20,2048]{2,1,0:T(8,128)(2,1)}), bf16[64,20,2048]{2,1,0:T(8,128)(2,1)}, u32[]{:S(2)}, u32[]{:S(2)}) async-start(bf16[64,20,2048]{2,1,0:T(8,128)(2,1)} %get-tuple-element.36), calls=%async_computation.1 | async-start | bytes 12582912 | tf_op jit(solution)/shard_map/all_to_all | solution.py:62
  235.5 386.9 %all-gather.2.cloned.1.call-start = ((), (), s32[]{:S(2)}) async-start(), calls=%async_computation.5 | async-start | bytes 26214400 | tf_op jit(solution)/shard_map/all_gather | solution.py:99
  395.2 7.4 copy-start.4
  407.7 0.8 copy-start.6
  443.3 202.0 %all-to-all-start.4 = ((bf16[64,1,20]{2,1,0:T(2,128)(2,1)}), bf16[64,1,20]{2,1,0:T(2,128)(2,1)S(1)}, u32[]{:S(2)}, u32[]{:S(2)}) async-start(bf16[64,1,20]{2,1,0:T(2,128)(2,1)} %copy.106), calls=%async_computation.4 | async-start | bytes 65536 | tf_op jit(solution)/shard_map/all_to_all | solution.py:108
  645.3 22.5 %slice-start = ((s8[5242880]{0:T(1024)(128)(4,1)}), s8[1048576]{0:T(1024)(128)(4,1)S(1)}, s32[]{:S(2)}) async-start(s8[5242880]{0:T(1024)(128)(4,1)} %bitcast.41), calls=%async_computation.6 | async-start | bytes 2097152
  645.3 152.1 %all-to-all-start.3 = ((bf16[64,20,2048]{2,1,0:T(8,128)(2,1)}), bf16[64,20,2048]{2,1,0:T(8,128)(2,1)}, u32[]{:S(2)}, u32[]{:S(2)}) async-start(bf16[64,20,2048]{2,1,0:T(8,128)(2,1)} %copy.104), calls=%async_computation.3 | async-start | bytes 12582912 | tf_op jit(solution)/shard_map/all_to_all | solution.py:105
  656.9 6.2 copy-start.8
  656.9 10.9 %slice-start.1 = ((s8[5242880]{0:T(1024)(128)(4,1)}), s8[4194304]{0:T(1024)(128)(4,1)S(1)}, s32[]{:S(2)}) async-start(s8[5242880]{0:T(1024)(128)(4,1)} %bitcast.41), calls=%async_computation.7 | async-start | bytes 8388608
  663.1 4.7 copy-start.7
  806.3 18.0 %copy-start.1 = (bf16[2,192,2048]{2,1,0:T(8,128)(2,1)S(1)}, bf16[2,192,2048]{2,1,0:T(8,128)(2,1)}, u32[]{:S(2)}) copy-start(bf16[2,192,2048]{2,1,0:T(8,128)(2,1)} %param.13) | copy-start | bytes 4718596
Sparse Core Ops, SparseCore 0:
  433.8 188.5 all-gather.1
